TPU v7x, 256 devices: a whole 4x4x8 slice. The times are simulated.
256 devices in a mesh: seq: 64 (over x, z, core), ch: 4 (over y).
Axes of the slice: x: 4, y: 4, z: 8, core: 2. Of those that a mesh axis runs over, the one named last changes fastest.
Arguments:
- proj: bfloat16 [3, 128, 65536], P(None, 'ch', 'seq'), may hold values from -6 to 6
- cotangent: bfloat16 [128, 65536], P('ch', 'seq'), may hold values from -6 to 6
- short_w: float32 [3, 128, 3], P(None, 'ch'), may hold values from -3.5 to 3.5
- filter_in: float32 [32, 64], replicated, may hold values from -5 to 5
- filter_out: float32 [64, 128], P(None, 'ch'), may hold values from -0.75 to 0.75
- rates: float32 [128], P('ch'), may hold values from 0.25 to 2184
Outputs:
- grad_proj: bfloat16 [3, 128, 65536], P(None, 'ch', 'seq')
- grad_short: float32 [3, 128, 3], P(None, 'ch')
- grad_filter_out: float32 [64, 128], P(None, 'ch')
- grad_filter_in: float32 [32, 64], replicated
All inputs are finite; a program needn't handle non-finite values.
Results may differ from a plain program's by a relative error of at most 0.0013.
Values may be sent and summed in bfloat16 or wider, within the bound.
A program may use at most 64 MiB of HBM per device.

v0:
```python
import math
import jax
import jax.numpy as jnp
from jax import lax
from jax.sharding import PartitionSpec as P

PRECISE = lax.Precision.HIGHEST


def shifted(value, axis, by):
    length = lax.axis_size(axis)
    pairs = [(i, i + by) for i in range(length) if 0 <= i + by < length]
    return lax.ppermute(value, axis, pairs)


def position_features(positions, length, feature_count):
    feature_index = jnp.arange(feature_count, dtype=jnp.int32)
    multiplier = (1 + feature_index // 2 * 499) % length
    upper = positions // 1024
    lower = positions % 1024
    phases = (
        upper[:, None] * (multiplier * 1024 % length)[None, :]
        + lower[:, None] * multiplier[None, :]
    ) % length
    angles = phases.astype(jnp.float32) * (2.0 * math.pi / length)
    return jnp.where((feature_index % 2 == 0)[None, :], jnp.cos(angles), jnp.sin(angles))


def angle_tables(row_count, col_count, row_start, col_start, modulus):
    row_index = row_start + jnp.arange(row_count, dtype=jnp.int32)
    col_index = col_start + jnp.arange(col_count, dtype=jnp.int32)
    phases = row_index[:, None] * col_index[None, :] % modulus
    angles = phases.astype(jnp.float32) * (2.0 * math.pi / modulus)
    return (jnp.cos(angles), jnp.sin(angles))


def rotate(real_part, imag_part, cosine, sine, sign):
    return (
        real_part * cosine - sign * imag_part * sine,
        imag_part * cosine + sign * real_part * sine,
    )


def dft_axis(real_part, imag_part, form, cosine, sine, sign):
    real_cos = jnp.einsum(form, real_part, cosine, precision=PRECISE)
    real_sin = jnp.einsum(form, real_part, sine, precision=PRECISE)
    imag_cos = jnp.einsum(form, imag_part, cosine, precision=PRECISE)
    imag_sin = jnp.einsum(form, imag_part, sine, precision=PRECISE)
    return (real_cos - sign * imag_sin, imag_cos + sign * real_sin)


def shards(proj, cotangent, short_w, filter_in, filter_out, rates):
    tap_count = short_w.shape[2]
    channels = proj.shape[1]
    devices = lax.axis_size("seq")
    tokens_here = proj.shape[2]
    length = devices * tokens_here
    modulus = 2 * length
    norm_scale = 1.0 / math.sqrt(length)
    column_width = tokens_here // devices
    first_split = math.gcd(tokens_here, 64)
    second_split = tokens_here // first_split
    device_index = lax.axis_index("seq")
    rim_cols = shifted(proj[:, :, tokens_here - (tap_count - 1) :], "seq", 1)
    extended = jnp.concatenate([rim_cols, proj], 2).astype(jnp.float32)

    def delayed(offset):
        return extended[:, :, tap_count - 1 - offset : tap_count - 1 - offset + tokens_here]

    mixed_all = short_w[:, :, 0, None] * delayed(0)
    for offset in range(1, tap_count):
        mixed_all = mixed_all + short_w[:, :, offset, None] * delayed(offset)
    query_part, key_part, value_part = (mixed_all[0], mixed_all[1], mixed_all[2])
    gated_prod = key_part * value_part
    cotangent_full = cotangent.astype(jnp.float32)
    grad_conv = cotangent_full * query_part
    both_signals = jnp.concatenate([gated_prod, grad_conv], 0).reshape(2 * channels, 1, tokens_here)
    columns = lax.all_to_all(both_signals, "seq", split_axis=2, concat_axis=1, tiled=True)
    block_start = jnp.arange(devices, dtype=jnp.int32) * tokens_here
    offset_start = device_index * column_width + jnp.arange(column_width, dtype=jnp.int32)
    column_pos = (block_start[:, None] + offset_start[None, :]).reshape(devices * column_width)
    features = position_features(column_pos, length, filter_in.shape[0])
    preact = jnp.dot(features, filter_in, precision=PRECISE, preferred_element_type=jnp.float32)
    hidden = jnp.sin(preact)
    modulated = jnp.einsum("to,oc->ct", hidden, filter_out, precision=PRECISE)
    relative = column_pos.astype(jnp.float32) / length
    spread = jnp.sqrt(jnp.expm1(-2.0 * rates) / jnp.expm1(-2.0 * rates / length))
    envelope = jnp.exp(-rates[:, None] * relative[None, :]) / spread[:, None]
    kernel = (envelope * modulated).reshape(channels, devices, column_width)
    stacked = jnp.concatenate([columns[:channels], kernel, columns[channels:]], 0)
    cos_outer, sin_outer = angle_tables(devices, 2 * devices, 0, 0, 2 * devices)
    turned_real = jnp.einsum("ran,ak->rkn", stacked, cos_outer, precision=PRECISE)
    turned_imag = -jnp.einsum("ran,ak->rkn", stacked, sin_outer, precision=PRECISE)
    cos_turn, sin_turn = angle_tables(
        2 * devices, column_width, 0, device_index * column_width, modulus
    )
    turned_real, turned_imag = rotate(turned_real, turned_imag, cos_turn, sin_turn, -1.0)
    moved_real, moved_imag = (
        lax.all_to_all(turned_real, "seq", split_axis=1, concat_axis=2, tiled=True),
        lax.all_to_all(turned_imag, "seq", split_axis=1, concat_axis=2, tiled=True),
    )
    row_total = moved_real.shape[0]
    cos_first, sin_first = angle_tables(first_split, first_split, 0, 0, first_split)
    cos_second, sin_second = angle_tables(second_split, second_split, 0, 0, second_split)
    cos_mid, sin_mid = angle_tables(first_split, second_split, 0, 0, tokens_here)
    grid_real = moved_real.reshape(row_total, 2, first_split, second_split)
    grid_imag = moved_imag.reshape(row_total, 2, first_split, second_split)
    grid_real, grid_imag = dft_axis(
        grid_real, grid_imag, "rkab,ac->rkcb", cos_first, sin_first, -1.0
    )
    grid_real, grid_imag = rotate(grid_real, grid_imag, cos_mid, sin_mid, -1.0)
    spec_real, spec_imag = dft_axis(
        grid_real, grid_imag, "rkcb,bd->rkcd", cos_second, sin_second, -1.0
    )
    gated_real, gated_imag = (spec_real[:channels], spec_imag[:channels])
    kernel_real, kernel_imag = (
        spec_real[channels : 2 * channels],
        spec_imag[channels : 2 * channels],
    )
    grad_real, grad_imag = (spec_real[2 * channels :], spec_imag[2 * channels :])
    conv_real = gated_real * kernel_real - gated_imag * kernel_imag
    conv_imag = gated_real * kernel_imag + gated_imag * kernel_real
    back_real = grad_real * kernel_real + grad_imag * kernel_imag
    back_imag = grad_imag * kernel_real - grad_real * kernel_imag
    kgrad_real = grad_real * gated_real + grad_imag * gated_imag
    kgrad_imag = grad_imag * gated_real - grad_real * gated_imag
    cos_back, sin_back = angle_tables(2, tokens_here, 2 * device_index, 0, modulus)
    cos_last, sin_last = angle_tables(2 * devices, devices, 0, 0, 2 * devices)
    real_part = jnp.concatenate([conv_real, back_real, kgrad_real], 0)
    rows = real_part.shape[0]
    part_real, part_imag = dft_axis(
        real_part,
        jnp.concatenate([conv_imag, back_imag, kgrad_imag], 0),
        "rkcd,db->rkcb",
        cos_second,
        sin_second,
        1.0,
    )
    part_real, part_imag = rotate(part_real, part_imag, cos_mid, sin_mid, 1.0)
    part_real, part_imag = dft_axis(
        part_real, part_imag, "rkcb,ca->rkab", cos_first, sin_first, 1.0
    )
    part_real = part_real.reshape(rows, 2, tokens_here)
    part_imag = part_imag.reshape(rows, 2, tokens_here)
    part_real, part_imag = rotate(part_real, part_imag, cos_back[None], sin_back[None], 1.0)
    spread_real = lax.all_to_all(part_real, "seq", split_axis=2, concat_axis=1, tiled=True)
    spread_imag = lax.all_to_all(part_imag, "seq", split_axis=2, concat_axis=1, tiled=True)
    real_out = jnp.einsum("rkn,ka->ran", spread_real, cos_last, precision=PRECISE)
    real_out = (real_out - jnp.einsum("rkn,ka->ran", spread_imag, sin_last, precision=PRECISE)) * (
        1.0 / modulus
    )
    conv_cols = real_out[:channels]
    gated_cols = real_out[channels : 2 * channels]
    kernel_grad = real_out[2 * channels :]
    returned = lax.all_to_all(
        jnp.concatenate([conv_cols, gated_cols], 0), "seq", split_axis=1, concat_axis=2, tiled=True
    )
    returned = returned.reshape(2 * channels, tokens_here)
    conv_out = returned[:channels]
    grad_gated = returned[channels:]
    grad_mixed = jnp.stack(
        [cotangent_full * conv_out, grad_gated * value_part, grad_gated * key_part]
    )
    short_part = jnp.stack(
        [jnp.sum(grad_mixed * delayed(offset), axis=2) for offset in range(tap_count)], axis=2
    )
    weighted = envelope * kernel_grad.reshape(channels, devices * column_width)
    out_part = jnp.einsum("to,ct->oc", hidden, weighted, precision=PRECISE)
    grad_hidden = jnp.einsum("ct,oc->to", weighted, filter_out, precision=PRECISE)
    in_part = jnp.einsum("tf,to->fo", features, grad_hidden * jnp.cos(preact), precision=PRECISE)
    next_rim = shifted(grad_mixed[:, :, : tap_count - 1], "seq", -1)
    grad_extended = jnp.concatenate([grad_mixed, next_rim], 2)
    result = short_w[:, :, 0, None] * grad_extended[:, :, 0:tokens_here]
    for offset in range(1, tap_count):
        result = (
            result
            + short_w[:, :, offset, None] * grad_extended[:, :, offset : offset + tokens_here]
        )
    grad_proj = result.astype(jnp.bfloat16)
    short_total, out_total = lax.psum((short_part, out_part), "seq")
    in_total = lax.psum(in_part, ("seq", "ch"))
    return (grad_proj, short_total * norm_scale, out_total * norm_scale, in_total * norm_scale)


def solution(mesh):
    placed = (
        P(None, "ch", "seq"),
        P("ch", "seq"),
        P(None, "ch", None),
        P(),
        P(None, "ch"),
        P("ch"),
    )
    return jax.shard_map(
        shards,
        mesh=mesh,
        in_specs=placed,
        out_specs=(P(None, "ch", "seq"), P(None, "ch", None), P(None, "ch"), P()),
        check_vma=False,
    )
```

profile of v0, /device:TPU:8, one launch (start us, length us, event | category | flops | bytes accessed | tf_op | source)
XLA Modules:
  0.0 598.5 jit_solution(10087766709720511439)
XLA Ops:
  4.3 5.1 fusion.244
  12.4 3.8 reduce
  16.2 2.1 reshape.320
  18.3 13.3 %all-to-all-start = ((f32[64,1,1024]{2,1,0:T(1,128)}), f32[64,1,1024]{2,1,0:T(1,128)}, u32[]{:S(2)}, u32[]{:S(2)}) async-start(f32[64,1,1024]{2,1,0:T(1,128)} %reshape.320), calls=%async_computation | async-start | bytes 524288 | tf_op jit(solution)/shard_map/all_to_all | solution.py:78
  37.6 5.8 all-to-all-done
  43.4 2.9 reduce.1
  46.4 2.4 reshape.321
  48.8 2.3 fusion.241
  53.9 2.9 add_bitcast_fusion.1
  56.9 2.5 copy.152
  59.4 6.3 %all-to-all-start.2 = ((f32[96,128,16]{0,2,1:T(8,128)}), f32[96,128,16]{0,2,1:T(8,128)}, u32[]{:S(2)}, u32[]{:S(2)}) async-start(f32[96,128,16]{0,2,1:T(8,128)} %copy.152), calls=%async_computation.2 | async-start | bytes 2097152 | tf_op jit(solution)/shard_map/all_to_all | solution.py:100
  65.6 2.5 copy.150
  68.2 25.5 %all-to-all-done.2 = f32[96,128,16]{0,2,1:T(8,128)} async-done(((f32[96,128,16]{0,2,1:T(8,128)}), f32[96,128,16]{0,2,1:T(8,128)}, u32[]{:S(2)}, u32[]{:S(2)}) %all-to-all-start.2) | async-done | bytes 786464 | tf_op jit(solution)/shard_map/all_to_all | solution.py:100
  93.7 7.2 %all-to-all-start.1 = ((f32[96,128,16]{0,2,1:T(8,128)}), f32[96,128,16]{0,2,1:T(8,128)}, u32[]{:S(2)}, u32[]{:S(2)}) async-start(f32[96,128,16]{0,2,1:T(8,128)} %copy.150), calls=%async_computation.1 | async-start | bytes 2097152 | tf_op jit(solution)/shard_map/all_to_all | solution.py:99
  101.4 3.8 fusion.14
  105.3 23.3 %all-to-all-done.1 = f32[96,128,16]{0,2,1:T(8,128)} async-done(((f32[96,128,16]{0,2,1:T(8,128)}), f32[96,128,16]{0,2,1:T(8,128)}, u32[]{:S(2)}, u32[]{:S(2)}) %all-to-all-start.1) | async-done | bytes 786464 | tf_op jit(solution)/shard_map/all_to_all | solution.py:99
  128.5 2.9 fusion.18
  131.5 2.9 fusion.7
  134.4 3.4 subtract_bitcast_fusion
  163.5 6.8 %all-to-all-start.3 = ((f32[96,2,1024]{0,1,2:T(2,128)}), f32[96,2,1024]{0,1,2:T(2,128)}, u32[]{:S(2)}, u32[]{:S(2)}) async-start(f32[96,2,1024]{0,1,2:T(2,128)} %copy.166), calls=%async_computation.3 | async-start | bytes 2097152 | tf_op jit(solution)/shard_map/all_to_all | solution.py:146
  170.4 3.0 copy.170
  173.4 25.0 %all-to-all-done.3 = f32[96,2,1024]{0,1,2:T(2,128)} async-done(((f32[96,2,1024]{0,1,2:T(2,128)}), f32[96,2,1024]{0,1,2:T(2,128)}, u32[]{:S(2)}, u32[]{:S(2)}) %all-to-all-start.3) | async-done | bytes 786464 | tf_op jit(solution)/shard_map/all_to_all | solution.py:146
  198.4 6.8 %all-to-all-start.4 = ((f32[96,2,1024]{0,1,2:T(2,128)}), f32[96,2,1024]{0,1,2:T(2,128)}, u32[]{:S(2)}, u32[]{:S(2)}) async-start(f32[96,2,1024]{0,1,2:T(2,128)} %copy.170), calls=%async_computation.4 | async-start | bytes 2097152 | tf_op jit(solution)/shard_map/all_to_all | solution.py:147
  208.5 24.7 %all-to-all-done.4 = f32[96,2,1024]{0,1,2:T(2,128)} async-done(((f32[96,2,1024]{0,1,2:T(2,128)}), f32[96,2,1024]{0,1,2:T(2,128)}, u32[]{:S(2)}, u32[]{:S(2)}) %all-to-all-start.4) | async-done | bytes 786464 | tf_op jit(solution)/shard_map/all_to_all | solution.py:147
  238.8 2.1 reshape.322
  240.9 7.0 %all-to-all-start.5 = ((f32[64,1,1024]{2,1,0:T(1,128)}), f32[64,1,1024]{2,1,0:T(1,128)}, u32[]{:S(2)}, u32[]{:S(2)}) async-start(f32[64,1,1024]{2,1,0:T(1,128)} %reshape.322), calls=%async_computation.5 | async-start | bytes 524288 | tf_op jit(solution)/shard_map/all_to_all | solution.py:155
  247.8 2.2 copy.175
  251.9 2.2 convolution_multiply_fusion.4
  254.1 3.0 fusion.43
  257.1 75.9 %psum.23 = f32[32,64]{1,0:T(8,128)S(1)} all-reduce(f32[32,64]{1,0:T(8,128)S(1)} %fusion.43), channel_id=1, replica_groups=mesh['seq'=64,'ch'=4] {'seq','ch'}, use_global_device_ids=true, to_apply=%region_5.6 | all-reduce | flops 2048 | bytes 16384 | tf_op jit(solution)/shard_map/psum | solution.py:181
  334.4 2.9 reduce.2
  346.4 250.5 %all-reduce = (f32[3,32,3]{1,0,2:T(4,128)S(1)}, f32[64,32]{0,1:T(8,128)S(1)}) all-reduce(f32[3,32,3]{1,0,2:T(4,128)S(1)} %pad_maximum_fusion.7, f32[64,32]{0,1:T(8,128)S(1)} %fusion.238), channel_id=1, replica_groups=mesh['seq'=64,'ch'=4] {'seq'}, use_global_device_ids=true, to_apply=%region_3.4 | all-reduce | flops 2336 | bytes 18688 | tf_op jit(solution)/shard_map/psum | solution.py:180
  (110 shorter events, 63.7 us)
Async XLA Ops:
  0.6 3.7 copy-start
  0.6 8.8 %copy-start.6 = (bf16[32,1024]{1,0:T(8,128)(2,1)S(1)}, bf16[32,1024]{1,0:T(8,128)(2,1)}, u32[]{:S(2)}) copy-start(bf16[32,1024]{1,0:T(8,128)(2,1)} %param.7) | copy-start | bytes 196612
  1.5 8.1 %collective-permute-start = (bf16[3,32,2]{2,1,0:T(8,128)(2,1)S(1)}, bf16[3,32,2]{2,1,0:T(8,128)(2,1)S(1)}, u32[]{:S(2)}, u32[]{:S(2)}) collective-permute-start(bf16[3,32,2]{2,1,0:T(8,128)(2,1)S(1)} %slice.96), channel_id=1, source_target_pairs={{0,4},{4,8},{8,12},{12,16},{16,20},{20,24},{24,28},{28,32},{32,36}... | collective-permute-start | bytes 1160 | tf_op jit(solution)/shard_map/ppermute | solution.py:13
  3.3 6.3 %copy-start.10 = (s32[32]{0:T(128)}, s32[32]{0:T(128)S(1)}, u32[]{:S(2)}) copy-start(s32[32]{0:T(128)S(1)} %get-tuple-element.66) | copy-start | bytes 388
  3.3 6.3 %copy-start.12 = (pred[32]{0:T(512)(128)(4,1)}, pred[32]{0:T(512)(128)(4,1)S(1)}, u32[]{:S(2)}) copy-start(pred[32]{0:T(512)(128)(4,1)S(1)} %fusion.143) | copy-start | bytes 100
  4.3 5.3 copy-start.5
  11.9 19.7 %copy-start.9 = (f32[32]{0:T(128)S(1)}, f32[32]{0:T(128)}, u32[]{:S(2)}) copy-start(f32[32]{0:T(128)} %param.11) | copy-start | bytes 388
  11.9 19.7 %copy-start.7 = (f32[64,32]{0,1:T(8,128)S(1)}, f32[64,32]{0,1:T(8,128)}, u32[]{:S(2)}) copy-start(f32[64,32]{0,1:T(8,128)} %param.10) | copy-start | bytes 24580
  18.3 25.2 %all-to-all-start = ((f32[64,1,1024]{2,1,0:T(1,128)}), f32[64,1,1024]{2,1,0:T(1,128)}, u32[]{:S(2)}, u32[]{:S(2)}) async-start(f32[64,1,1024]{2,1,0:T(1,128)} %reshape.320), calls=%async_computation | async-start | bytes 524288 | tf_op jit(solution)/shard_map/all_to_all | solution.py:78
  51.1 1.0 copy-start.2
  59.4 34.3 %all-to-all-start.2 = ((f32[96,128,16]{0,2,1:T(8,128)}), f32[96,128,16]{0,2,1:T(8,128)}, u32[]{:S(2)}, u32[]{:S(2)}) async-start(f32[96,128,16]{0,2,1:T(8,128)} %copy.152), calls=%async_computation.2 | async-start | bytes 2097152 | tf_op jit(solution)/shard_map/all_to_all | solution.py:100
  93.7 34.9 %all-to-all-start.1 = ((f32[96,128,16]{0,2,1:T(8,128)}), f32[96,128,16]{0,2,1:T(8,128)}, u32[]{:S(2)}, u32[]{:S(2)}) async-start(f32[96,128,16]{0,2,1:T(8,128)} %copy.150), calls=%async_computation.1 | async-start | bytes 2097152 | tf_op jit(solution)/shard_map/all_to_all | solution.py:99
  128.5 3.0 copy-start.3
  163.5 34.9 %all-to-all-start.3 = ((f32[96,2,1024]{0,1,2:T(2,128)}), f32[96,2,1024]{0,1,2:T(2,128)}, u32[]{:S(2)}, u32[]{:S(2)}) async-start(f32[96,2,1024]{0,1,2:T(2,128)} %copy.166), calls=%async_computation.3 | async-start | bytes 2097152 | tf_op jit(solution)/shard_map/all_to_all | solution.py:146
  198.4 34.9 %all-to-all-start.4 = ((f32[96,2,1024]{0,1,2:T(2,128)}), f32[96,2,1024]{0,1,2:T(2,128)}, u32[]{:S(2)}, u32[]{:S(2)}) async-start(f32[96,2,1024]{0,1,2:T(2,128)} %copy.170), calls=%async_computation.4 | async-start | bytes 2097152 | tf_op jit(solution)/shard_map/all_to_all | solution.py:147
  234.5 1.0 copy-start.4
  238.8 13.1 %copy-start.8 = (f32[64,32]{0,1:T(8,128)S(1)}, f32[64,32]{0,1:T(8,128)}, u32[]{:S(2)}) copy-start(f32[64,32]{0,1:T(8,128)} %param.10) | copy-start | bytes 24580
  240.9 13.2 %copy-start.11 = (s32[32]{0:T(128)S(1)}, s32[32]{0:T(128)}, u32[]{:S(2)}) copy-start(s32[32]{0:T(128)} %copy-done.10) | copy-start | bytes 388
  240.9 13.2 %copy-start.13 = (pred[32]{0:T(512)(128)(4,1)S(1)}, pred[32]{0:T(512)(128)(4,1)}, u32[]{:S(2)}) copy-start(pred[32]{0:T(512)(128)(4,1)} %copy-done.12) | copy-start | bytes 100
  240.9 93.6 %all-to-all-start.5 = ((f32[64,1,1024]{2,1,0:T(1,128)}), f32[64,1,1024]{2,1,0:T(1,128)}, u32[]{:S(2)}, u32[]{:S(2)}) async-start(f32[64,1,1024]{2,1,0:T(1,128)} %reshape.322), calls=%async_computation.5 | async-start | bytes 524288 | tf_op jit(solution)/shard_map/all_to_all | solution.py:155
  341.0 3.1 collective-permute-start.1
  344.1 253.9 %copy-start.1 = (f32[32,64]{1,0:T(8,128)S(1)}, f32[32,64]{1,0:T(8,128)}, u32[]{:S(2)}) copy-start(f32[32,64]{1,0:T(8,128)} %param.9) | copy-start | bytes 24580
where the time goes:
time: 605 us; the launch traced here: 599 us
  blocking collectives  326 us (54%)
  waiting for transfers between devices  106 us (18%)
  matrix products  52.9 us (9%)
  starting transfers between devices  50.4 us (8%)
  local copies, waits for them, and re-layouts  42.8 us (7%)
  other arithmetic  18.9 us (3%)
    psum x1, blocking collectives, shards(): short_total, out_total = lax.psum((short_part, out_part), 'seq')  250 us
    psum x1, blocking collectives, shards(): in_total = lax.psum(in_part, ('seq', 'ch'))  75.9 us
    all_to_all x1, waiting for transfers between devices, shards(): lax.all_to_all(turned_imag, 'seq', split_axis=1, concat_axis=2, tiled=True)  25.5 us
    all_to_all x1, waiting for transfers between devices, shards(): lax.all_to_all(part_real, 'seq', split_axis=2, concat_axis=1, tiled=True)  25 us
    all_to_all x1, waiting for transfers between devices, shards(): lax.all_to_all(part_imag, 'seq', split_axis=2, concat_axis=1, tiled=True)  24.7 us
    all_to_all x1, waiting for transfers between devices, shards(): lax.all_to_all(turned_real, 'seq', split_axis=1, concat_axis=2, tiled=True)  23.3 us
    all_to_all x1, starting transfers between devices, shards(): lax.all_to_all(both_signals, 'seq', split_axis=2, concat_axis=1, tiled=True)  13.3 us
    unnamed x38, local copies, waits for them, and re-layouts  12.3 us
  transfers between devices with their start and end apart: 8, of which 6 were waited for; matrix products, arithmetic and copies ran while one was open for 6% of the time, Pallas kernels for 0%

commit v1 on v0

--- a/solution.py
+++ b/solution.py
@@ -178,7 +178,7 @@
         )
     grad_proj = result.astype(jnp.bfloat16)
     short_total, out_total = lax.psum((short_part, out_part), "seq")
-    in_total = lax.psum(in_part, ("seq", "ch"))
+    in_total = lax.psum(lax.psum(in_part, "ch"), "seq")
     return (grad_proj, short_total * norm_scale, out_total * norm_scale, in_total * norm_scale)
 
 

time: 605 us -> 544 us (0.90)
  blocking collectives: 326 us -> 261 us
    psum x1, blocking collectives: 75.9 us -> 14.1 us  [shards(): in_total = lax.psum(lax.psum(in_part, 'ch'), 'seq')]
    unnamed x38 -> x50, local copies, waits for them, and re-layouts: 12.3 us -> 14.4 us
  transfers between devices with their start and end apart: 8 -> 8, of which waited for: 6 -> 6; matrix products, arithmetic and copies ran while one was open for 6% -> 7% of each run, Pallas kernels for 0% -> 0%
where the time goes in v1:
time: 544 us; the launch traced here: 537 us
  blocking collectives  261 us (48%)
  waiting for transfers between devices  106 us (19%)
  matrix products  52 us (10%)
  starting transfers between devices  50.4 us (9%)
  local copies, waits for them, and re-layouts  44.8 us (8%)
  other arithmetic  21 us (4%)
    psum x1, blocking collectives, shards(): short_total, out_total = lax.psum((short_part, out_part), 'seq')  246 us
    all_to_all x1, waiting for transfers between devices, shards(): lax.all_to_all(turned_imag, 'seq', split_axis=1, concat_axis=2, tiled=True)  25.5 us
    all_to_all x1, waiting for transfers between devices, shards(): lax.all_to_all(part_real, 'seq', split_axis=2, concat_axis=1, tiled=True)  25 us
    all_to_all x1, waiting for transfers between devices, shards(): lax.all_to_all(part_imag, 'seq', split_axis=2, concat_axis=1, tiled=True)  24.7 us
    all_to_all x1, waiting for transfers between devices, shards(): lax.all_to_all(turned_real, 'seq', split_axis=1, concat_axis=2, tiled=True)  23.3 us
    unnamed x50, local copies, waits for them, and re-layouts  14.4 us
    psum x1, blocking collectives, shards(): in_total = lax.psum(lax.psum(in_part, 'ch'), 'seq')  14.1 us
    all_to_all x1, starting transfers between devices, shards(): lax.all_to_all(both_signals, 'seq', split_axis=2, concat_axis=1, tiled=True)  13.3 us
  transfers between devices with their start and end apart: 8, of which 6 were waited for; matrix products, arithmetic and copies ran while one was open for 7% of the time, Pallas kernels for 0%

profile of v1, /device:TPU:8, one launch (start us, length us, event | category | flops | bytes accessed | tf_op | source)
XLA Modules:
  0.0 537.0 jit_solution(1288926309835482088)
XLA Ops:
  4.3 5.1 fusion.244
  12.4 3.8 reduce
  18.3 13.3 %all-to-all-start = ((f32[64,1,1024]{2,1,0:T(1,128)}), f32[64,1,1024]{2,1,0:T(1,128)}, u32[]{:S(2)}, u32[]{:S(2)}) async-start(f32[64,1,1024]{2,1,0:T(1,128)} %reshape.320), calls=%async_computation | async-start | bytes 524288 | tf_op jit(solution)/shard_map/all_to_all | solution.py:78
  37.6 5.8 %all-to-all-done = f32[64,1,1024]{2,1,0:T(1,128)} async-done(((f32[64,1,1024]{2,1,0:T(1,128)}), f32[64,1,1024]{2,1,0:T(1,128)}, u32[]{:S(2)}, u32[]{:S(2)}) %all-to-all-start) | async-done | bytes 262176 | tf_op jit(solution)/shard_map/all_to_all | solution.py:78
  43.5 2.9 reduce.1
  46.4 2.4 reshape.321
  48.9 2.3 fusion.241
  54.0 2.9 add_bitcast_fusion.1
  56.9 2.5 copy.152
  59.4 6.3 %all-to-all-start.2 = ((f32[96,128,16]{0,2,1:T(8,128)}), f32[96,128,16]{0,2,1:T(8,128)}, u32[]{:S(2)}, u32[]{:S(2)}) async-start(f32[96,128,16]{0,2,1:T(8,128)} %copy.152), calls=%async_computation.2 | async-start | bytes 2097152 | tf_op jit(solution)/shard_map/all_to_all | solution.py:100
  65.7 2.5 copy.150
  68.2 25.5 %all-to-all-done.2 = f32[96,128,16]{0,2,1:T(8,128)} async-done(((f32[96,128,16]{0,2,1:T(8,128)}), f32[96,128,16]{0,2,1:T(8,128)}, u32[]{:S(2)}, u32[]{:S(2)}) %all-to-all-start.2) | async-done | bytes 786464 | tf_op jit(solution)/shard_map/all_to_all | solution.py:100
  93.7 7.2 %all-to-all-start.1 = ((f32[96,128,16]{0,2,1:T(8,128)}), f32[96,128,16]{0,2,1:T(8,128)}, u32[]{:S(2)}, u32[]{:S(2)}) async-start(f32[96,128,16]{0,2,1:T(8,128)} %copy.150), calls=%async_computation.1 | async-start | bytes 2097152 | tf_op jit(solution)/shard_map/all_to_all | solution.py:99
  101.5 3.8 fusion.14
  105.3 23.3 %all-to-all-done.1 = f32[96,128,16]{0,2,1:T(8,128)} async-done(((f32[96,128,16]{0,2,1:T(8,128)}), f32[96,128,16]{0,2,1:T(8,128)}, u32[]{:S(2)}, u32[]{:S(2)}) %all-to-all-start.1) | async-done | bytes 786464 | tf_op jit(solution)/shard_map/all_to_all | solution.py:99
  128.6 2.9 fusion.18
  131.5 2.9 fusion.7
  134.5 3.4 subtract_bitcast_fusion
  163.6 6.8 %all-to-all-start.3 = ((f32[96,2,1024]{0,1,2:T(2,128)}), f32[96,2,1024]{0,1,2:T(2,128)}, u32[]{:S(2)}, u32[]{:S(2)}) async-start(f32[96,2,1024]{0,1,2:T(2,128)} %copy.166), calls=%async_computation.3 | async-start | bytes 2097152 | tf_op jit(solution)/shard_map/all_to_all | solution.py:146
  170.4 3.0 copy.170
  173.4 25.0 %all-to-all-done.3 = f32[96,2,1024]{0,1,2:T(2,128)} async-done(((f32[96,2,1024]{0,1,2:T(2,128)}), f32[96,2,1024]{0,1,2:T(2,128)}, u32[]{:S(2)}, u32[]{:S(2)}) %all-to-all-start.3) | async-done | bytes 786464 | tf_op jit(solution)/shard_map/all_to_all | solution.py:146
  198.4 6.8 %all-to-all-start.4 = ((f32[96,2,1024]{0,1,2:T(2,128)}), f32[96,2,1024]{0,1,2:T(2,128)}, u32[]{:S(2)}, u32[]{:S(2)}) async-start(f32[96,2,1024]{0,1,2:T(2,128)} %copy.170), calls=%async_computation.4 | async-start | bytes 2097152 | tf_op jit(solution)/shard_map/all_to_all | solution.py:147
  208.6 24.7 %all-to-all-done.4 = f32[96,2,1024]{0,1,2:T(2,128)} async-done(((f32[96,2,1024]{0,1,2:T(2,128)}), f32[96,2,1024]{0,1,2:T(2,128)}, u32[]{:S(2)}, u32[]{:S(2)}) %all-to-all-start.4) | async-done | bytes 786464 | tf_op jit(solution)/shard_map/all_to_all | solution.py:147
  238.8 2.1 reshape.322
  240.9 7.0 %all-to-all-start.5 = ((f32[64,1,1024]{2,1,0:T(1,128)}), f32[64,1,1024]{2,1,0:T(1,128)}, u32[]{:S(2)}, u32[]{:S(2)}) async-start(f32[64,1,1024]{2,1,0:T(1,128)} %reshape.322), calls=%async_computation.5 | async-start | bytes 524288 | tf_op jit(solution)/shard_map/all_to_all | solution.py:155
  247.9 2.2 copy.175
  251.9 2.3 convolution_multiply_fusion.4
  254.2 3.0 fusion.43
  259.7 2.9 reduce.2
  268.4 14.1 %psum.30 = f32[32,64]{1,0:T(8,128)S(1)} all-reduce(f32[32,64]{1,0:T(8,128)S(1)} %fusion.43), channel_id=1, replica_groups=mesh['seq'=64,'ch'=4] {'ch'}, use_global_device_ids=true, to_apply=%region_5.6 | all-reduce | flops 2048 | bytes 16384 | tf_op jit(solution)/shard_map/psum | solution.py:181
  284.1 2.1 multiply_reduce_fusion.2
  288.2 246.5 %all-reduce = (f32[3,32,3]{1,0,2:T(4,128)S(1)}, f32[64,32]{0,1:T(8,128)S(1)}, f32[32,64]{1,0:T(8,128)S(1)}) all-reduce(f32[3,32,3]{1,0,2:T(4,128)S(1)} %pad_maximum_fusion.7, f32[64,32]{0,1:T(8,128)S(1)} %fusion.238, f32[32,64]{1,0:T(8,128)S(1)} %psum.30), channel_id=1, replica_groups=mesh['seq'=64,'ch'=4] {'seq'}, use_global_device_ids=true, to_apply=%region_3.4 | all-reduce | flops 4384 | bytes 35072 | tf_op jit(solution)/shard_map/psum | solution.py:180
  (122 shorter events, 67.7 us)
Async XLA Ops:
  0.6 3.7 copy-start
  0.6 8.8 %copy-start.11 = (bf16[32,1024]{1,0:T(8,128)(2,1)S(1)}, bf16[32,1024]{1,0:T(8,128)(2,1)}, u32[]{:S(2)}) copy-start(bf16[32,1024]{1,0:T(8,128)(2,1)} %param.7) | copy-start | bytes 196612
  1.5 8.2 %collective-permute-start = (bf16[3,32,2]{2,1,0:T(8,128)(2,1)S(1)}, bf16[3,32,2]{2,1,0:T(8,128)(2,1)S(1)}, u32[]{:S(2)}, u32[]{:S(2)}) collective-permute-start(bf16[3,32,2]{2,1,0:T(8,128)(2,1)S(1)} %slice.96), channel_id=1, source_target_pairs={{0,4},{4,8},{8,12},{12,16},{16,20},{20,24},{24,28},{28,32},{32,36}... | collective-permute-start | bytes 1160 | tf_op jit(solution)/shard_map/ppermute | solution.py:13
  3.3 6.4 %copy-start.15 = (s32[32]{0:T(128)}, s32[32]{0:T(128)S(1)}, u32[]{:S(2)}) copy-start(s32[32]{0:T(128)S(1)} %get-tuple-element.67) | copy-start | bytes 388
  3.3 6.3 %copy-start.17 = (pred[32]{0:T(512)(128)(4,1)}, pred[32]{0:T(512)(128)(4,1)S(1)}, u32[]{:S(2)}) copy-start(pred[32]{0:T(512)(128)(4,1)S(1)} %fusion.143) | copy-start | bytes 100
  4.3 5.3 copy-start.9
  11.9 19.7 %copy-start.14 = (f32[32]{0:T(128)S(1)}, f32[32]{0:T(128)}, u32[]{:S(2)}) copy-start(f32[32]{0:T(128)} %param.11) | copy-start | bytes 388
  11.9 19.8 %copy-start.12 = (f32[64,32]{0,1:T(8,128)S(1)}, f32[64,32]{0,1:T(8,128)}, u32[]{:S(2)}) copy-start(f32[64,32]{0,1:T(8,128)} %param.10) | copy-start | bytes 24580
  18.3 25.2 %all-to-all-start = ((f32[64,1,1024]{2,1,0:T(1,128)}), f32[64,1,1024]{2,1,0:T(1,128)}, u32[]{:S(2)}, u32[]{:S(2)}) async-start(f32[64,1,1024]{2,1,0:T(1,128)} %reshape.320), calls=%async_computation | async-start | bytes 524288 | tf_op jit(solution)/shard_map/all_to_all | solution.py:78
  51.2 1.0 copy-start.6
  59.4 34.3 %all-to-all-start.2 = ((f32[96,128,16]{0,2,1:T(8,128)}), f32[96,128,16]{0,2,1:T(8,128)}, u32[]{:S(2)}, u32[]{:S(2)}) async-start(f32[96,128,16]{0,2,1:T(8,128)} %copy.152), calls=%async_computation.2 | async-start | bytes 2097152 | tf_op jit(solution)/shard_map/all_to_all | solution.py:100
  93.7 34.9 %all-to-all-start.1 = ((f32[96,128,16]{0,2,1:T(8,128)}), f32[96,128,16]{0,2,1:T(8,128)}, u32[]{:S(2)}, u32[]{:S(2)}) async-start(f32[96,128,16]{0,2,1:T(8,128)} %copy.150), calls=%async_computation.1 | async-start | bytes 2097152 | tf_op jit(solution)/shard_map/all_to_all | solution.py:99
  128.6 3.0 copy-start.7
  163.6 34.9 %all-to-all-start.3 = ((f32[96,2,1024]{0,1,2:T(2,128)}), f32[96,2,1024]{0,1,2:T(2,128)}, u32[]{:S(2)}, u32[]{:S(2)}) async-start(f32[96,2,1024]{0,1,2:T(2,128)} %copy.166), calls=%async_computation.3 | async-start | bytes 2097152 | tf_op jit(solution)/shard_map/all_to_all | solution.py:146
  198.4 34.9 %all-to-all-start.4 = ((f32[96,2,1024]{0,1,2:T(2,128)}), f32[96,2,1024]{0,1,2:T(2,128)}, u32[]{:S(2)}, u32[]{:S(2)}) async-start(f32[96,2,1024]{0,1,2:T(2,128)} %copy.170), calls=%async_computation.4 | async-start | bytes 2097152 | tf_op jit(solution)/shard_map/all_to_all | solution.py:147
  234.6 1.0 copy-start.8
  238.8 13.1 %copy-start.13 = (f32[64,32]{0,1:T(8,128)S(1)}, f32[64,32]{0,1:T(8,128)}, u32[]{:S(2)}) copy-start(f32[64,32]{0,1:T(8,128)} %param.10) | copy-start | bytes 24580
  240.9 13.3 %copy-start.16 = (s32[32]{0:T(128)S(1)}, s32[32]{0:T(128)}, u32[]{:S(2)}) copy-start(s32[32]{0:T(128)} %copy-done.15) | copy-start | bytes 388
  240.9 13.3 %copy-start.18 = (pred[32]{0:T(512)(128)(4,1)S(1)}, pred[32]{0:T(512)(128)(4,1)}, u32[]{:S(2)}) copy-start(pred[32]{0:T(512)(128)(4,1)} %copy-done.17) | copy-start | bytes 100
  240.9 18.8 %all-to-all-start.5 = ((f32[64,1,1024]{2,1,0:T(1,128)}), f32[64,1,1024]{2,1,0:T(1,128)}, u32[]{:S(2)}, u32[]{:S(2)}) async-start(f32[64,1,1024]{2,1,0:T(1,128)} %reshape.322), calls=%async_computation.5 | async-start | bytes 524288 | tf_op jit(solution)/shard_map/all_to_all | solution.py:155
  251.9 5.3 copy-start.10
  251.9 5.3 copy-start.19
  266.1 0.8 copy-start.2
  266.1 1.0 copy-start.4
  267.1 15.4 %collective-permute-start.1 = (f32[3,32,2]{1,2,0:T(2,128)S(1)}, f32[3,32,2]{1,2,0:T(2,128)S(1)}, u32[]{:S(2)}, u32[]{:S(2)}) collective-permute-start(f32[3,32,2]{1,2,0:T(2,128)S(1)} %slice.139), channel_id=1, source_target_pairs={{4,0},{8,4},{12,8},{16,12},{20,16},{24,20},{28,24},{32,28},{36,32}... | collective-permute-start | bytes 2312 | tf_op jit(solution)/shard_map/ppermute | solution.py:13
  282.5 1.4 copy-start.3
  282.5 1.5 copy-start.5
  284.1 252.5 %copy-start.1 = (f32[32,64]{1,0:T(8,128)S(1)}, f32[32,64]{1,0:T(8,128)}, u32[]{:S(2)}) copy-start(f32[32,64]{1,0:T(8,128)} %param.9) | copy-start | bytes 24580
